TPU v7x, 512 devices: a whole 4x8x8 slice. The times are simulated.
512 devices in a mesh: tm: 64 (over y_hi, z, core), chan: 8 (over y_lo, x).
Axes of the slice: x: 4, y: 8 (y_hi: 4, y_lo: 2; y = y_hi * 2 + y_lo), z: 8, core: 2. Of those that a mesh axis runs over, the one named last changes fastest.
Arguments:
- samples: bfloat16 [32768, 4096], P('tm', 'chan'), may hold values from -6 to 6
- sketch: bfloat16 [4, 4096, 256], P(None, 'chan'), may hold values from -0.046875 to 0.046875
Outputs:
- image: float32 [8, 512, 4, 256], P('chan', 'tm')
All inputs are finite; a program needn't handle non-finite values.
Results may differ from a plain program's by a relative error of at most 0.0029.
Values may be sent and summed in bfloat16 or wider, within the bound.
No kernel may reach another device: no remote copies, remote signals or barrier semaphores. Data moves between devices by JAX's collectives and lax.ppermute only.
A program may use at most 64 MiB of HBM per device.

v0:
```python
import jax
import jax.numpy as jnp
from jax import lax
from jax.sharding import PartitionSpec as P


def from_behind(block, axis, distance):
    devices = range(lax.axis_size(axis))
    route = [(i - distance, i) for i in devices if i - distance in devices]
    return lax.ppermute(block, axis, route)


def cut_along(array, dim, devices):
    before, after = (array.shape[:dim], array.shape[dim + 1 :])
    return jnp.moveaxis(array.reshape(*before, devices, -1, *after), dim, 0)


def summed_on_arrival(array, axis, dim):
    pieces = cut_along(array, dim, lax.axis_size(axis))
    arrived = lax.all_to_all(pieces, axis, split_axis=0, concat_axis=0, tiled=True)
    return arrived.sum(axis=0)


def shards(samples, sketch):
    rows, local = samples.shape
    blocks = sketch.shape[0]
    span = 2 * blocks - 1
    ahead = from_behind(samples[:span], "tm", -1)
    padded = jnp.concatenate([samples, ahead], 0)
    partial_proj = jnp.einsum("tc,jcr->tjr", samples, sketch, preferred_element_type=jnp.float32)
    proj = lax.psum(partial_proj, "chan")
    proj = proj.astype(jnp.bfloat16)
    groups = lax.axis_size("tm")
    share = local // groups
    scale_factor = 1.0 / jnp.sqrt(jnp.float32(rows * groups))
    results = []
    for row_block in range(blocks):
        windows = jnp.stack(
            [
                lax.dynamic_slice(
                    padded, (blocks + row_block - column, 0), (rows, share * lax.axis_size("tm"))
                )
                for column in range(blocks)
            ]
        )
        results.append(
            lax.dot_general(
                windows, proj, (((0, 1), (1, 0)), ((), ())), preferred_element_type=jnp.float32
            )
        )
    mine = summed_on_arrival(jnp.stack(results, 1), "tm", 0)
    return (mine * scale_factor)[None]


def solution(mesh):
    placed = (P("tm", "chan"), P(None, "chan", None))
    return jax.shard_map(
        shards, mesh=mesh, in_specs=placed, out_specs=P("chan", "tm", None, None), check_vma=False
    )
```

profile of v0, /device:TPU:101, one launch (start us, length us, event | category | flops | bytes accessed | tf_op | source)
XLA Modules:
  0.0 168.2 jit_solution(13555997833428660455)
XLA Ops:
  0.0 0.0 copy-start
  0.0 0.8 slice.3
  0.8 0.2 copy.5
  1.0 2.6 %collective-permute-start = (bf16[7,512]{0,1:T(8,128)(2,1)S(1)}, bf16[7,512]{0,1:T(8,128)(2,1)S(1)}, u32[]{:S(2)}, u32[]{:S(2)}) collective-permute-start(bf16[7,512]{0,1:T(8,128)(2,1)S(1)} %copy.5), channel_id=1, source_target_pairs={{8,0},{16,8},{24,16},{32,24},{40,32},{48,40},{56,48},{64,56},{72,6... | collective-permute-start | bytes 21512 | tf_op jit(solution)/shard_map/ppermute | solution.py:10
  3.6 0.0 copy-done
  3.6 1.8 %fusion.57 = f32[512,4,256]{2,0,1:T(8,128)S(1)} fusion(bf16[4,512,256]{2,1,0:T(8,128)(2,1)S(1)} %copy-done, bf16[512,512]{1,0:T(8,128)(2,1)} %param.2), kind=kOutput, calls=%fused_computation.63 | convolution fusion | flops 536870912 | bytes 3670016 | tf_op jit(solution)/shard_map/tc,jcr->tjr/dot_general | solution.py:30
  5.3 60.3 %all-reduce.1 = bf16[512,4,256]{2,0,1:T(8,128)(2,1)} all-reduce(f32[512,4,256]{2,0,1:T(8,128)S(1)} %fusion.57), channel_id=1, replica_groups=mesh['tm'=64,'chan'=8] {'chan'}, use_global_device_ids=true, to_apply=%region_0.0 | all-reduce | flops 524288 | bytes 3145728 | tf_op jit(solution)/shard_map/psum | solution.py:31
  65.7 1.3 copy.6
  66.9 0.0 copy-start.1
  66.9 0.0 collective-permute-done
  67.0 2.1 %fusion.53 = (bf16[1,512,512]{1,2,0:T(8,128)(2,1)S(1)}, bf16[1,512,512]{1,2,0:T(8,128)(2,1)S(1)}, bf16[1,512,512]{1,2,0:T(8,128)(2,1)S(1)}, bf16[1,512,512]{1,2,...) fusion(bf16[512,512]{0,1:T(8,128)(2,1)S(1)} %copy.6, ...), kind=kLoop, calls=%fused_computation.58 | loop fusion | flops 7340032 | bytes 4201472 | tf_op jit(solution)/shard_map/stack | solution.py:38
  69.0 0.0 copy-done.1
  69.1 0.7 fusion.41
  69.8 0.7 fusion.38
  70.5 0.7 fusion.35
  71.2 0.7 fusion.32
  71.9 0.2 pad_maximum_fusion
  72.1 95.3 %all_to_all.5 = f32[64,8,4,256]{3,1,2,0:T(8,128)S(1)} all-to-all(f32[64,8,4,256]{3,1,2,0:T(8,128)S(1)} %pad_maximum_fusion), channel_id=1, replica_groups=mesh['tm'=64,'chan'=8] {'tm'}, dimensions={0} | all-to-all | bytes 4194304 | tf_op jit(solution)/shard_map/all_to_all | solution.py:20
  167.4 0.1 reduce_sum.9
  167.5 0.6 copy.12
  (1 shorter events, 0.0 us)
Async XLA Ops:
  0.0 3.6 %copy-start = (bf16[4,512,256]{2,1,0:T(8,128)(2,1)S(1)}, bf16[4,512,256]{2,1,0:T(8,128)(2,1)}, u32[]{:S(2)}) copy-start(bf16[4,512,256]{2,1,0:T(8,128)(2,1)} %param.3) | copy-start | bytes 3145732
  1.0 66.0 %collective-permute-start = (bf16[7,512]{0,1:T(8,128)(2,1)S(1)}, bf16[7,512]{0,1:T(8,128)(2,1)S(1)}, u32[]{:S(2)}, u32[]{:S(2)}) collective-permute-start(bf16[7,512]{0,1:T(8,128)(2,1)S(1)} %copy.5), channel_id=1, source_target_pairs={{8,0},{16,8},{24,16},{32,24},{40,32},{48,40},{56,48},{64,56},{72,6... | collective-permute-start | bytes 21512 | tf_op jit(solution)/shard_map/ppermute | solution.py:10
  66.9 2.1 %copy-start.1 = (bf16[512,4,256]{2,0,1:T(8,128)(2,1)S(1)}, bf16[512,4,256]{2,0,1:T(8,128)(2,1)}, u32[]{:S(2)}) copy-start(bf16[512,4,256]{2,0,1:T(8,128)(2,1)} %all-reduce.1) | copy-start | bytes 3145732
where the time goes:
time: 168 us
  blocking collectives  156 us (93%)
  matrix products  4.6 us (3%)
  local copies, waits for them, and re-layouts  2.85 us (2%)
  starting transfers between devices  2.58 us (2%)
  other arithmetic  2.4 us (1%)
    all_to_all x1, blocking collectives, summed_on_arrival(): lax.all_to_all(pieces, axis, split_axis=0, concat_axis=0, tiled=True)  95.3 us
    psum x1, blocking collectives, shards(): proj = lax.psum(partial_proj, 'chan')  60.3 us
  transfers between devices with their start and end apart: 1, of which 0 were waited for; matrix products, arithmetic and copies ran while one was open for 2% of the time, Pallas kernels for 0%

commit v1 on v0

v1 whole, which is shorter than its diff:
```python
import functools

import jax
import jax.numpy as jnp
from jax import lax
from jax.experimental import pallas as pl
from jax.experimental.pallas import tpu as pltpu
from jax.sharding import Mesh
from jax.sharding import PartitionSpec as P

TM = ("y_hi", "z", "core")
CHAN = ("y_lo", "x")
EDGE = 8
LANES = 128


def in_vmem(kernel, out_shape, scratch=()):
    whole = pl.BlockSpec(memory_space=pltpu.VMEM)
    return lambda *args: pl.pallas_call(
        kernel,
        out_shape=out_shape,
        in_specs=[whole] * len(args),
        out_specs=whole,
        scratch_shapes=list(scratch),
        name=kernel.func.__name__ if isinstance(kernel, functools.partial) else kernel.__name__,
    )(*args)


def exchanged(pieces, axis):
    return lax.all_to_all(pieces, axis, split_axis=0, concat_axis=0, tiled=True)


def sketched(samples_ref, sketch_ref, out_ref, held):
    blocks = sketch_ref.shape[0]
    rows = samples_ref.shape[0]
    reach = out_ref.shape[0]
    for j in range(blocks):
        held[j, :EDGE] = jnp.zeros((EDGE, held.shape[2]), jnp.float32)
        held[j, EDGE + rows :] = jnp.zeros((held.shape[1] - EDGE - rows, held.shape[2]), jnp.float32)
        held[j, EDGE : EDGE + rows] = jnp.dot(
            samples_ref[...], sketch_ref[j], preferred_element_type=jnp.float32
        )
    total = held[blocks - 1, EDGE : EDGE + reach]
    for j in range(blocks - 1):
        start = EDGE - (blocks - 1 - j)
        total = total + held[j, start : start + reach]
    out_ref[...] = total


def copied(arrived_ref, out_ref):
    total = arrived_ref[0]
    for i in range(1, arrived_ref.shape[0]):
        total = total + arrived_ref[i]
    halves, copies, _, width = out_ref.shape
    for h in range(halves):
        for k in range(copies):
            out_ref[h, k] = total[:, h * width : (h + 1) * width]


def correlated(block_rows, rows, scale, turned_ref, sums_ref, out_ref, held):
    width = sums_ref.shape[2]
    reach = sums_ref.shape[1]
    depth = turned_ref.shape[1]
    held[...] = jnp.zeros_like(held)
    held[EDGE : EDGE + reach] = sums_ref[0]
    for k in range(1, sums_ref.shape[0]):
        start = EDGE + k * rows
        held[start : start + reach] = held[start : start + reach] + sums_ref[k]
    for i in range(block_rows):
        wide = held[EDGE - 1 - i : EDGE - 1 - i + depth]
        high = wide.astype(jnp.bfloat16)
        low = (wide - high.astype(jnp.float32)).astype(jnp.bfloat16)
        found = jnp.dot(turned_ref[...], high, preferred_element_type=jnp.float32)
        found = found + jnp.dot(turned_ref[...], low, preferred_element_type=jnp.float32)
        out_ref[:, i * width : (i + 1) * width] = (found * scale).astype(out_ref.dtype)


def shards(samples, sketch):
    rows, local = samples.shape
    blocks, _, width = sketch.shape
    cores = lax.axis_size("core")
    near = lax.axis_size(CHAN)
    groups = lax.axis_size(TM)
    half = width // cores
    part = -(-(rows + blocks - 1) // (near * EDGE)) * EDGE
    reach = near * part
    depth = cores * rows + 2 * EDGE

    other = lax.ppermute(samples, "core", [(i, cores - 1 - i) for i in range(cores)])
    first = lax.axis_index("core") == 0
    chip = jnp.where(
        first, jnp.concatenate([samples, other], 0), jnp.concatenate([other, samples], 0)
    )
    ahead = lax.ppermute(chip[:EDGE], TM, [(i + cores, i) for i in range(groups - cores)])
    tail = jnp.zeros((depth - cores * rows - EDGE, local), samples.dtype)
    turned = jnp.concatenate([chip, ahead, tail], 0).T

    partial = in_vmem(
        sketched,
        jax.ShapeDtypeStruct((reach, width), jnp.float32),
        [pltpu.VMEM((blocks, reach + 2 * EDGE, width), jnp.float32)],
    )(samples, sketch)
    arrived = exchanged(partial.reshape(near, part, width), CHAN)
    copies = in_vmem(copied, jax.ShapeDtypeStruct((cores, near, part, half), jnp.float32))(arrived)
    sums = exchanged(copies.reshape(cores * near, part, half), ("core", *CHAN))
    scale = 1.0 / (rows * groups) ** 0.5
    found = in_vmem(
        functools.partial(correlated, blocks, rows, scale),
        jax.ShapeDtypeStruct((local, blocks * half), jnp.bfloat16),
        [pltpu.VMEM((EDGE + (cores - 1) * rows + reach + 2 * EDGE, half), jnp.float32)],
    )(turned, sums.reshape(cores, reach, half))
    landed = exchanged(found.reshape(groups, local // groups, blocks * half), TM)
    landed = landed.reshape(groups // cores, cores, local // groups, blocks, half)
    mine = landed.astype(jnp.float32).sum(0)
    return jnp.moveaxis(mine, 0, 2).reshape(1, local // groups, blocks, width)


def solution(mesh):
    sizes = {"y_hi": 4, "z": 8, "core": 2, "y_lo": 2, "x": 4}
    fine = Mesh(mesh.devices.reshape(tuple(sizes.values())), tuple(sizes))
    placed = (P(TM, CHAN), P(None, CHAN, None))
    return jax.shard_map(
        shards, mesh=fine, in_specs=placed, out_specs=P(CHAN, TM, None, None), check_vma=False
    )
```

time: 168 us -> 87.4 us (0.52)
  the two profiles are of different devices: /device:TPU:101 before, /device:TPU:1 now
where the time goes in v1:
time: 87.4 us; the launch traced here: 86.9 us
  blocking collectives  52.7 us (60%)
  starting transfers between devices  13 us (15%)
  Pallas kernels  9.82 us (11%)
  waiting for transfers between devices  7.18 us (8%)
  local copies, waits for them, and re-layouts  3.74 us (4%)
    all_to_all x2, blocking collectives, exchanged(): return lax.all_to_all(pieces, axis, split_axis=0, concat_axis=0, tiled=True)  52.7 us
    pallas_call x3, Pallas kernels, in_vmem(): pl.pallas_call(kernel, out_shape=out_shape, in_specs=[whole] * len(args),...  9.82 us
    all_to_all x1, starting transfers between devices, exchanged(): return lax.all_to_all(pieces, axis, split_axis=0, concat_axis=0, tiled=True)  9.63 us
    ppermute x1, waiting for transfers between devices, shards(): lax.ppermute(chip[:EDGE], TM, [(i + cores, i) for i in range(groups - cor...  5.47 us
    ppermute x1, starting transfers between devices, shards(): lax.ppermute(samples, 'core', [(i, cores - 1 - i) for i in range(cores)])  2.08 us
    concatenate x1, local copies, waits for them, and re-layouts, shards(): turned = jnp.concatenate([chip, ahead, tail], 0).T  1.93 us
  transfers between devices with their start and end apart: 3, of which 2 were waited for; matrix products, arithmetic and copies ran while one was open for 3% of the time, Pallas kernels for 0%

profile of v1, /device:TPU:1, one launch (start us, length us, event | category | flops | bytes accessed | tf_op | source)
XLA Modules:
  0.0 86.9 jit_solution(1660255478086798762)
XLA Ops:
  0.0 2.9 %sketched.1 = f32[576,256]{1,0:T(8,128)} custom-call(bf16[512,512]{1,0:T(8,128)(2,1)} %samples_ref.1, bf16[4,512,256]{2,1,0:T(8,128)(2,1)} %sketch_ref.1), custom_call_target="tpu_custom_call" | custom-call | tf_op jit(solution)/shard_map/sketched/pallas_call | solution.py:19
  2.9 14.0 %all_to_all.15.arrived_ref = f32[8,72,256]{2,1,0:T(8,128)} all-to-all(f32[8,72,256]{2,1,0:T(8,128)} %bitcast.11), channel_id=1, replica_groups=mesh['y_hi'=4,'z'=8,'core'=2,'y_lo'=2,'x'=4] {'y_lo','x'}, dimensions={0} | all-to-all | bytes 1179648 | tf_op jit(solution)/shard_map/all_to_all | solution.py:30
  16.9 0.0 copy-start.1
  16.9 2.0 %copied.1 = f32[2,8,72,128]{3,2,1,0:T(8,128)} custom-call(f32[8,72,256]{2,1,0:T(8,128)} %all_to_all.15.arrived_ref), custom_call_target="tpu_custom_call" | custom-call | tf_op jit(solution)/shard_map/copied/pallas_call | solution.py:19
  18.9 9.6 %all-to-all-start.1 = ((f32[16,72,128]{2,1,0:T(8,128)}), f32[16,72,128]{2,1,0:T(8,128)S(1)}, u32[]{:S(2)}, u32[]{:S(2)}) async-start(f32[16,72,128]{2,1,0:T(8,128)} %bitcast.10), calls=%async_computation.1 | async-start | bytes 1179648 | tf_op jit(solution)/shard_map/all_to_all | solution.py:30
  28.5 0.0 copy-done.1
  28.5 0.2 copy.10
  28.8 2.1 %collective-permute-start = (bf16[512,512]{0,1:T(8,128)(2,1)S(1)}, bf16[512,512]{0,1:T(8,128)(2,1)S(1)}, u32[]{:S(2)}, u32[]{:S(2)}) collective-permute-start(bf16[512,512]{0,1:T(8,128)(2,1)S(1)} %copy.10), channel_id=1, source_target_pairs={{0,8},{8,0},{1,9},{9,1},{2,10},{10,2},{3,11},{11,3},{4,12},{12,4},... | collective-permute-start | bytes 1572872 | tf_op jit(solution)/shard_map/ppermute | solution.py:89
  30.9 1.7 %collective-permute-done = bf16[512,512]{0,1:T(8,128)(2,1)S(1)} collective-permute-done((bf16[512,512]{0,1:T(8,128)(2,1)S(1)}, bf16[512,512]{0,1:T(8,128)(2,1)S(1)}, u32[]{:S(2)}, u32[]{:S(2)}) %collective-permute-start) | collective-permute-done | bytes 524320 | tf_op jit(solution)/shard_map/ppermute | solution.py:89
  32.6 0.3 maximum_select_fusion
  32.9 1.3 %collective-permute-start.1 = (bf16[8,512]{0,1:T(8,128)(2,1)S(1)}, bf16[8,512]{0,1:T(8,128)(2,1)S(1)}, u32[]{:S(2)}, u32[]{:S(2)}) collective-permute-start(bf16[8,512]{0,1:T(8,128)(2,1)S(1)} %slice.4), channel_id=1, source_target_pairs={{16,0},{24,8},{32,16},{40,24},{48,32},{56,40},{64,48},{72,56},{80,... | collective-permute-start | bytes 24584 | tf_op jit(solution)/shard_map/ppermute | solution.py:94
  34.2 5.5 %collective-permute-done.1 = bf16[8,512]{0,1:T(8,128)(2,1)S(1)} collective-permute-done((bf16[8,512]{0,1:T(8,128)(2,1)S(1)}, bf16[8,512]{0,1:T(8,128)(2,1)S(1)}, u32[]{:S(2)}, u32[]{:S(2)}) %collective-permute-start.1) | collective-permute-done | bytes 8224 | tf_op jit(solution)/shard_map/ppermute | solution.py:94
  39.7 1.9 %concatenate.11 = bf16[1040,512]{0,1:T(8,128)(2,1)} concatenate(bf16[1024,512]{0,1:T(8,128)(2,1)S(1)} %maximum_select_fusion, bf16[8,512]{0,1:T(8,128)(2,1)S(1)} %collective-permute-done.1, bf16[8,512]{0,1:T(8,128)(2,1)S(1)} %broadcast_in_dim.3), dimensions={0} | concatenate | bytes 2129920 | tf_op jit(solution)/shard_map/concatenate | solution.py:96
  41.6 0.0 all-to-all-done.1
  41.7 0.0 copy-start
  41.7 0.9 copy-done
  42.5 4.9 %correlated.1 = bf16[512,512]{1,0:T(8,128)(2,1)} custom-call(bf16[512,1040]{1,0:T(8,128)(2,1)} %bitcast.8, f32[2,576,128]{2,1,0:T(8,128)} %bitcast.9), custom_call_target="tpu_custom_call" | custom-call | tf_op jit(solution)/shard_map/correlated/pallas_call | solution.py:19
  47.4 38.7 %all_to_all.16 = bf16[64,8,512]{2,1,0:T(8,128)(2,1)S(1)} all-to-all(bf16[64,8,512]{2,1,0:T(8,128)(2,1)} %bitcast.13), channel_id=1, replica_groups=mesh['y_hi'=4,'z'=8,'core'=2,'y_lo'=2,'x'=4] {'y_hi','z','core'}, dimensions={0} | all-to-all | bytes 1048576 | tf_op jit(solution)/shard_map/all_to_all | solution.py:30
  86.1 0.1 convert_reduce_fusion
  86.3 0.6 reshape.24
  (3 shorter events, 0.1 us)
Async XLA Ops:
  16.9 11.7 %copy-start.1 = (bf16[512,512]{1,0:T(8,128)(2,1)S(1)}, bf16[512,512]{1,0:T(8,128)(2,1)}, u32[]{:S(2)}) copy-start(bf16[512,512]{1,0:T(8,128)(2,1)} %samples_ref.1) | copy-start | bytes 1572868
  18.9 22.7 %all-to-all-start.1 = ((f32[16,72,128]{2,1,0:T(8,128)}), f32[16,72,128]{2,1,0:T(8,128)S(1)}, u32[]{:S(2)}, u32[]{:S(2)}) async-start(f32[16,72,128]{2,1,0:T(8,128)} %bitcast.10), calls=%async_computation.1 | async-start | bytes 1179648 | tf_op jit(solution)/shard_map/all_to_all | solution.py:30
  28.8 3.8 %collective-permute-start = (bf16[512,512]{0,1:T(8,128)(2,1)S(1)}, bf16[512,512]{0,1:T(8,128)(2,1)S(1)}, u32[]{:S(2)}, u32[]{:S(2)}) collective-permute-start(bf16[512,512]{0,1:T(8,128)(2,1)S(1)} %copy.10), channel_id=1, source_target_pairs={{0,8},{8,0},{1,9},{9,1},{2,10},{10,2},{3,11},{11,3},{4,12},{12,4},... | collective-permute-start | bytes 1572872 | tf_op jit(solution)/shard_map/ppermute | solution.py:89
  32.9 6.8 %collective-permute-start.1 = (bf16[8,512]{0,1:T(8,128)(2,1)S(1)}, bf16[8,512]{0,1:T(8,128)(2,1)S(1)}, u32[]{:S(2)}, u32[]{:S(2)}) collective-permute-start(bf16[8,512]{0,1:T(8,128)(2,1)S(1)} %slice.4), channel_id=1, source_target_pairs={{16,0},{24,8},{32,16},{40,24},{48,32},{56,40},{64,48},{72,56},{80,... | collective-permute-start | bytes 24584 | tf_op jit(solution)/shard_map/ppermute | solution.py:94
  41.7 0.9 copy-start

commit v2 on v1

v2 whole, which is shorter than its diff:
```python
import functools

import jax
import jax.numpy as jnp
from jax import lax
from jax.experimental import pallas as pl
from jax.experimental.pallas import tpu as pltpu
from jax.sharding import Mesh
from jax.sharding import PartitionSpec as P

TM = ("y_hi", "z", "core")
CHAN = ("y_lo", "x")
EDGE = 8
ROOT_SCALE = 512.0


def in_vmem(name, kernel, out_shape, scratch=()):
    whole = pl.BlockSpec(memory_space=pltpu.VMEM)
    return lambda *args: pl.pallas_call(
        kernel,
        out_shape=out_shape,
        in_specs=[whole] * len(args),
        out_specs=whole,
        scratch_shapes=list(scratch),
        name=name,
    )(*args)


def exchanged(pieces, axis):
    return lax.all_to_all(pieces, axis, split_axis=0, concat_axis=0, tiled=True)


def coded(values):
    root = jnp.sqrt(jnp.abs(values)) * ROOT_SCALE
    return jnp.where(values < 0, -root, root).astype(jnp.float16)


def decoded(codes):
    root = codes.astype(jnp.float32) * (1.0 / ROOT_SCALE)
    return root * jnp.abs(root)


def sketched(samples_ref, sketch_ref, out_ref, held):
    blocks = sketch_ref.shape[0]
    rows = samples_ref.shape[0]
    reach = out_ref.shape[0]
    for j in range(blocks):
        held[j, :EDGE] = jnp.zeros((EDGE, held.shape[2]), jnp.float32)
        held[j, EDGE + rows :] = jnp.zeros((held.shape[1] - EDGE - rows, held.shape[2]), jnp.float32)
        held[j, EDGE : EDGE + rows] = jnp.dot(
            samples_ref[...], sketch_ref[j], preferred_element_type=jnp.float32
        )
    total = held[blocks - 1, EDGE : EDGE + reach]
    for j in range(blocks - 1):
        start = EDGE - (blocks - 1 - j)
        total = total + held[j, start : start + reach]
    out_ref[...] = total


def correlated(block_rows, scale, own_ref, other_ref, tail_ref, sums_ref, out_ref, held, high, low):
    cores, reach, width = sums_ref.shape
    rows = own_ref.shape[1]
    depth = high.shape[0]
    held[...] = jnp.zeros_like(held)
    held[EDGE : EDGE + reach] = sums_ref[0]
    for k in range(1, cores):
        start = EDGE + k * rows
        held[start : start + reach] = held[start : start + reach] + sums_ref[k]
    for i in range(block_rows):
        wide = held[EDGE - 1 - i : EDGE - 1 - i + depth]
        part = wide.astype(jnp.bfloat16)
        high[:, i * width : (i + 1) * width] = part
        low[:, i * width : (i + 1) * width] = (wide - part.astype(jnp.float32)).astype(jnp.bfloat16)
    core = lax.axis_index("core")
    mine = pl.ds(pl.multiple_of(core * rows, rows), rows)
    theirs = pl.ds(pl.multiple_of((cores - 1 - core) * rows, rows), rows)
    ends = pl.ds(cores * rows, depth - cores * rows)
    found = jnp.zeros(out_ref.shape, jnp.float32)
    for turned, where in ((own_ref, mine), (other_ref, theirs), (tail_ref, ends)):
        for sums in (high, low):
            found = found + jnp.dot(turned[...], sums[where], preferred_element_type=jnp.float32)
    out_ref[...] = (found * scale).astype(out_ref.dtype)


def landed_sum(block_rows, landed_ref, out_ref):
    senders, cores, _, length = landed_ref.shape
    half = length // block_rows
    for k in range(cores):
        total = landed_ref[0, k].astype(jnp.float32)
        for n in range(1, senders):
            total = total + landed_ref[n, k].astype(jnp.float32)
        for i in range(block_rows):
            out_ref[0, :, i, k * half : (k + 1) * half] = total[:, i * half : (i + 1) * half]


def shards(samples, sketch):
    rows, local = samples.shape
    blocks, _, width = sketch.shape
    cores = lax.axis_size("core")
    near = lax.axis_size(CHAN)
    groups = lax.axis_size(TM)
    half = width // cores
    part = -(-(rows + blocks - 1) // (near * EDGE)) * EDGE
    reach = near * part
    depth = cores * rows + 2 * EDGE

    with jax.named_scope("head"):
        route = [(i + 1, i) for i in range(cores - 1, groups - 1, cores)]
        head = lax.ppermute(samples[:EDGE], TM, route)
    with jax.named_scope("sketched"):
        partial = in_vmem(
            "sketched",
            sketched,
            jax.ShapeDtypeStruct((reach, width), jnp.float32),
            [pltpu.VMEM((blocks, reach + 2 * EDGE, width), jnp.float32)],
        )(samples, sketch)
    partial, head = lax.optimization_barrier((partial, head))
    with jax.named_scope("swap"):
        swap = [(i, cores - 1 - i) for i in range(cores)]
        other = lax.ppermute(jnp.concatenate([samples, head], 0), "core", swap)
    with jax.named_scope("reduce"):
        arrived = exchanged(coded(partial).reshape(near, part, width), CHAN)
    arrived, other = lax.optimization_barrier((arrived, other))
    total = coded(decoded(arrived).sum(0))
    copies = [
        jnp.broadcast_to(total[None, :, k * half : (k + 1) * half], (near, part, half))
        for k in range(cores)
    ]
    with jax.named_scope("gather"):
        sums = exchanged(jnp.concatenate(copies, 0), ("core", *CHAN))
    first = lax.axis_index("core") == 0
    tail = jnp.where(first, other[rows:], head)
    tail = jnp.pad(tail, ((0, depth - cores * rows - EDGE), (0, 0)))
    scale = 1.0 / (rows * groups) ** 0.5
    found = in_vmem(
        "correlated",
        functools.partial(correlated, blocks, scale),
        jax.ShapeDtypeStruct((local, blocks * half), jnp.bfloat16),
        [
            pltpu.VMEM((EDGE + (cores - 1) * rows + reach + 2 * EDGE, half), jnp.float32),
            pltpu.VMEM((depth, blocks * half), jnp.bfloat16),
            pltpu.VMEM((depth, blocks * half), jnp.bfloat16),
        ],
    )(samples.T, other[:rows].T, tail.T, decoded(sums).reshape(cores, reach, half))
    with jax.named_scope("scatter"):
        landed = exchanged(found.reshape(groups, local // groups, blocks * half), TM)
    return in_vmem(
        "landed",
        functools.partial(landed_sum, blocks),
        jax.ShapeDtypeStruct((1, local // groups, blocks, width), jnp.float32),
    )(landed.reshape(groups // cores, cores, local // groups, blocks * half))


def solution(mesh):
    sizes = {"y_hi": 4, "z": 8, "core": 2, "y_lo": 2, "x": 4}
    fine = Mesh(mesh.devices.reshape(tuple(sizes.values())), tuple(sizes))
    placed = (P(TM, CHAN), P(None, CHAN, None))
    return jax.shard_map(
        shards, mesh=fine, in_specs=placed, out_specs=P(CHAN, TM, None, None), check_vma=False
    )
```

time: 87.4 us -> 83.6 us (0.957)
  blocking collectives: 52.7 us -> 37 us
  waiting for transfers between devices: 7.18 us -> 15.6 us
  other arithmetic: 0.38 us -> 2.85 us
  starting transfers between devices: 13 us -> 14.6 us
  Pallas kernels: 9.82 us -> 8.88 us
    all_to_all x2 -> x1, blocking collectives: 52.7 us -> 37 us  [exchanged(): return lax.all_to_all(pieces, axis, split_axis=0, concat_axis=0, tiled=True)]
    all_to_all x1 -> x2, waiting for transfers between devices: 0.01 us -> 12.4 us  [exchanged(): return lax.all_to_all(pieces, axis, split_axis=0, concat_axis=0, tiled=True)]
    ppermute x2, waiting for transfers between devices: 7.18 us -> 3.17 us  [the longest x1 3.17 us: shards(): head = lax.ppermute(samples[:EDGE], TM, route)]
    ppermute x2, starting transfers between devices: 3.38 us -> 6.51 us  [the longest x1 5.09 us: shards(): other = lax.ppermute(jnp.concatenate([samples, head], 0), 'core', swap)]
    concatenate x1 -> x0, local copies, waits for them, and re-layouts: 1.93 us -> none  [shards(): turned = jnp.concatenate([chip, ahead, tail], 0).T]
    all_to_all x1 -> x2, starting transfers between devices: 9.63 us -> 8.06 us  [exchanged(): return lax.all_to_all(pieces, axis, split_axis=0, concat_axis=0, tiled=True)]
    transpose x0 -> x2, local copies, waits for them, and re-layouts: none -> 1.55 us  [the longest x1 0.87 us: shards(): other[:rows]]
    convert_element_type x0 -> x2, other arithmetic: none -> 1 us  [coded(): return jnp.where(values < 0, -root, root).astype(jnp.float16)]
  transfers between devices with their start and end apart: 3 -> 4, of which waited for: 2 -> 3; matrix products, arithmetic and copies ran while one was open for 3% -> 4% of each run, Pallas kernels for 0% -> 4%
where the time goes in v2:
time: 83.6 us; the launch traced here: 83.1 us
  blocking collectives  37 us (44%)
  waiting for transfers between devices  15.6 us (19%)
  starting transfers between devices  14.6 us (17%)
  Pallas kernels  8.88 us (11%)
  local copies, waits for them, and re-layouts  4 us (5%)
  other arithmetic  2.85 us (3%)
    all_to_all x1, blocking collectives, exchanged(): return lax.all_to_all(pieces, axis, split_axis=0, concat_axis=0, tiled=True)  37 us
    all_to_all x2, waiting for transfers between devices, exchanged(): return lax.all_to_all(pieces, axis, split_axis=0, concat_axis=0, tiled=True)  12.4 us
    pallas_call x3, Pallas kernels, in_vmem(): pl.pallas_call(kernel, out_shape=out_shape, in_specs=[whole] * len(args),...  8.88 us
    all_to_all x2, starting transfers between devices, exchanged(): return lax.all_to_all(pieces, axis, split_axis=0, concat_axis=0, tiled=True)  8.06 us
    ppermute x1, starting transfers between devices, shards(): other = lax.ppermute(jnp.concatenate([samples, head], 0), 'core', swap)  5.09 us
    ppermute x1, waiting for transfers between devices, shards(): head = lax.ppermute(samples[:EDGE], TM, route)  3.17 us
  transfers between devices with their start and end apart: 4, of which 3 were waited for; matrix products, arithmetic and copies ran while one was open for 4% of the time, Pallas kernels for 4%

profile of v2, /device:TPU:1, one launch (start us, length us, event | category | flops | bytes accessed | tf_op | source)
XLA Modules:
  0.0 83.1 jit_solution(15030620900652020492)
XLA Ops:
  0.0 0.7 slice.15
  0.7 0.2 copy.7
  0.9 0.0 copy-start
  0.9 1.4 %collective-permute-start = (bf16[8,512]{0,1:T(8,128)(2,1)S(1)}, bf16[8,512]{0,1:T(8,128)(2,1)S(1)}, u32[]{:S(2)}, u32[]{:S(2)}) collective-permute-start(bf16[8,512]{0,1:T(8,128)(2,1)S(1)} %copy.7), channel_id=1, source_target_pairs={{16,8},{32,24},{48,40},{64,56},{80,72},{96,88},{112,104},{128,120}... | collective-permute-start | bytes 24584 | tf_op jit(solution)/shard_map/head/ppermute | solution.py:109
  2.3 2.9 %sketched.1 = f32[576,256]{1,0:T(8,128)} custom-call(bf16[512,512]{1,0:T(8,128)(2,1)} %samples_ref.1, bf16[4,512,256]{2,1,0:T(8,128)(2,1)} %sketch_ref.1), custom_call_target="tpu_custom_call" | custom-call | tf_op jit(solution)/shard_map/sketched/sketched/pallas_call | solution.py:19
  5.2 3.2 %collective-permute-done = bf16[8,512]{0,1:T(8,128)(2,1)S(1)} collective-permute-done((bf16[8,512]{0,1:T(8,128)(2,1)S(1)}, bf16[8,512]{0,1:T(8,128)(2,1)S(1)}, u32[]{:S(2)}, u32[]{:S(2)}) %collective-permute-start) | collective-permute-done | bytes 8224 | tf_op jit(solution)/shard_map/head/ppermute | solution.py:109
  8.4 0.1 copy.8
  8.5 5.1 %collective-permute-start.1 = (bf16[520,512]{1,0:T(8,128)(2,1)S(1)}, bf16[520,512]{1,0:T(8,128)(2,1)S(1)}, u32[]{:S(2)}, u32[]{:S(2)}) collective-permute-start(bf16[520,512]{1,0:T(8,128)(2,1)S(1)} %pad_maximum_fusion), channel_id=1, source_target_pairs={{0,8},{8,0},{1,9},{9,1},{2,10},{10,2},{3,11},{11,3},{4,12},{12,4},... | collective-permute-start | bytes 1597448 | tf_op jit(solution)/shard_map/swap/ppermute | solution.py:120
  13.6 1.0 %fusion = f16[576,256]{1,0:T(8,128)(2,1)} fusion(f32[576,256]{1,0:T(8,128)S(1)} %copy-done.1), kind=kLoop, calls=%fused_computation.3 | loop fusion | flops 884736 | bytes 884736 | tf_op jit(solution)/shard_map/reduce/convert_element_type | solution.py:35
  14.6 3.4 %all-to-all-start = ((f16[8,72,256]{2,1,0:T(8,128)(2,1)}), f16[8,72,256]{2,1,0:T(8,128)(2,1)S(1)}, u32[]{:S(2)}, u32[]{:S(2)}) async-start(f16[8,72,256]{2,1,0:T(8,128)(2,1)} %bitcast.1), calls=%async_computation | async-start | bytes 589824 | tf_op jit(solution)/shard_map/reduce/all_to_all | solution.py:30
  18.0 1.0 %copy.6 = bf16[512,512]{0,1:T(8,128)(2,1)} copy(bf16[512,512]{1,0:T(8,128)(2,1)S(1)} %copy-done) | data formatting | bytes 1048576 | tf_op args[0]
  19.0 5.9 %all-to-all-done = f16[8,72,256]{2,1,0:T(8,128)(2,1)S(1)} async-done(((f16[8,72,256]{2,1,0:T(8,128)(2,1)}), f16[8,72,256]{2,1,0:T(8,128)(2,1)S(1)}, u32[]{:S(2)}, u32[]{:S(2)}) %all-to-all-start) | async-done | bytes 294944 | tf_op jit(solution)/shard_map/reduce/all_to_all | solution.py:30
  24.9 0.3 copy.9
  25.2 0.1 fusion.1
  25.4 0.2 copy.10
  25.6 0.8 pad_maximum_fusion.1
  26.4 4.6 %all-to-all-start.1 = ((f16[16,72,128]{2,1,0:T(8,128)(2,1)}), f16[16,72,128]{2,1,0:T(8,128)(2,1)S(1)}, u32[]{:S(2)}, u32[]{:S(2)}) async-start(f16[16,72,128]{2,1,0:T(8,128)(2,1)} %pad_maximum_fusion.1), calls=%async_computation.1 | async-start | bytes 589824 | tf_op jit(solution)/shard_map/gather/all_to_all | solution.py:30
  31.1 0.7 pad_bitcast_fusion.tail_ref
  31.8 0.9 %slice_bitcast_fusion.other_ref = bf16[512,512]{1,0:T(8,128)(2,1)} fusion(bf16[520,512]{0,1:T(8,128)(2,1)S(1)} %copy.9), kind=kLoop, calls=%fused_computation.6 | loop fusion | bytes 1048576 | tf_op jit(solution)/shard_map/transpose | solution.py:144
  32.6 6.5 %all-to-all-done.1 = f16[16,72,128]{2,1,0:T(8,128)(2,1)S(1)} async-done(((f16[16,72,128]{2,1,0:T(8,128)(2,1)}), f16[16,72,128]{2,1,0:T(8,128)(2,1)S(1)}, u32[]{:S(2)}, u32[]{:S(2)}) %all-to-all-start.1) | async-done | bytes 294944 | tf_op jit(solution)/shard_map/gather/all_to_all | solution.py:30
  39.2 0.9 %abs_multiply_fusion = f32[16,72,128]{2,1,0:T(8,128)} fusion(f16[16,72,128]{2,1,0:T(8,128)(2,1)S(1)} %all-to-all-done.1), kind=kLoop, calls=%fused_computation | loop fusion | flops 589824 | bytes 884736 | tf_op jit(solution)/shard_map/mul | solution.py:40
  40.1 4.2 %correlated.1 = bf16[512,512]{1,0:T(8,128)(2,1)} custom-call(bf16[512,512]{1,0:T(8,128)(2,1)} %bitcast.11, bf16[512,512]{1,0:T(8,128)(2,1)} %slice_bitcast_fusion.other_ref, bf16[512,16]{1,0:T(8,128)(2,1)} %pad_bitcast_fusion.tail_ref, f32[2,576,128]{2,1,0:T(8,128)} %bitcast.9), custom_call_target="tpu_custom_call" | custom-call | tf_op jit(solution)/shard_map/correlated/pallas_call | solution.py:19
  44.3 37.0 %all_to_all.15 = bf16[64,8,512]{2,1,0:T(8,128)(2,1)} all-to-all(bf16[64,8,512]{2,1,0:T(8,128)(2,1)} %bitcast.12), channel_id=1, replica_groups=mesh['y_hi'=4,'z'=8,'core'=2,'y_lo'=2,'x'=4] {'y_hi','z','core'}, dimensions={0} | all-to-all | bytes 1048576 | tf_op jit(solution)/shard_map/scatter/all_to_all | solution.py:30
  81.3 1.8 %landed.1 = f32[1,8,4,256]{3,2,1,0:T(4,128)} custom-call(bf16[32,2,8,512]{3,2,1,0:T(8,128)(2,1)} %bitcast.10), custom_call_target="tpu_custom_call" | custom-call | tf_op jit(solution)/shard_map/landed/pallas_call | solution.py:19
  (11 shorter events, 0.2 us)
Async XLA Ops:
  0.9 7.6 %copy-start = (bf16[512,512]{1,0:T(8,128)(2,1)S(1)}, bf16[512,512]{1,0:T(8,128)(2,1)}, u32[]{:S(2)}) copy-start(bf16[512,512]{1,0:T(8,128)(2,1)} %samples_ref.1) | copy-start | bytes 1572868
  0.9 7.5 %collective-permute-start = (bf16[8,512]{0,1:T(8,128)(2,1)S(1)}, bf16[8,512]{0,1:T(8,128)(2,1)S(1)}, u32[]{:S(2)}, u32[]{:S(2)}) collective-permute-start(bf16[8,512]{0,1:T(8,128)(2,1)S(1)} %copy.7), channel_id=1, source_target_pairs={{16,8},{32,24},{48,40},{64,56},{80,72},{96,88},{112,104},{128,120}... | collective-permute-start | bytes 24584 | tf_op jit(solution)/shard_map/head/ppermute | solution.py:109
  5.2 8.4 %copy-start.1 = (f32[576,256]{1,0:T(8,128)S(1)}, f32[576,256]{1,0:T(8,128)}, u32[]{:S(2)}) copy-start(f32[576,256]{1,0:T(8,128)} %sketched.1) | copy-start | bytes 1769476
  8.5 16.4 %collective-permute-start.1 = (bf16[520,512]{1,0:T(8,128)(2,1)S(1)}, bf16[520,512]{1,0:T(8,128)(2,1)S(1)}, u32[]{:S(2)}, u32[]{:S(2)}) collective-permute-start(bf16[520,512]{1,0:T(8,128)(2,1)S(1)} %pad_maximum_fusion), channel_id=1, source_target_pairs={{0,8},{8,0},{1,9},{9,1},{2,10},{10,2},{3,11},{11,3},{4,12},{12,4},... | collective-permute-start | bytes 1597448 | tf_op jit(solution)/shard_map/swap/ppermute | solution.py:120
  14.6 10.3 %all-to-all-start = ((f16[8,72,256]{2,1,0:T(8,128)(2,1)}), f16[8,72,256]{2,1,0:T(8,128)(2,1)S(1)}, u32[]{:S(2)}, u32[]{:S(2)}) async-start(f16[8,72,256]{2,1,0:T(8,128)(2,1)} %bitcast.1), calls=%async_computation | async-start | bytes 589824 | tf_op jit(solution)/shard_map/reduce/all_to_all | solution.py:30
  26.4 12.7 %all-to-all-start.1 = ((f16[16,72,128]{2,1,0:T(8,128)(2,1)}), f16[16,72,128]{2,1,0:T(8,128)(2,1)S(1)}, u32[]{:S(2)}, u32[]{:S(2)}) async-start(f16[16,72,128]{2,1,0:T(8,128)(2,1)} %pad_maximum_fusion.1), calls=%async_computation.1 | async-start | bytes 589824 | tf_op jit(solution)/shard_map/gather/all_to_all | solution.py:30

commit v3 on v2

v3 whole, which is shorter than its diff:
```python
import functools

import jax
import jax.numpy as jnp
from jax import lax
from jax.experimental import pallas as pl
from jax.experimental.layout import Layout, with_layout_constraint
from jax.experimental.pallas import tpu as pltpu
from jax.sharding import Mesh
from jax.sharding import PartitionSpec as P

TM = ("y_hi", "z", "core")
CHAN = ("y_lo", "x")
EDGE = 8
LANES = 128
ROOT_SCALE = 512.0
ANY = pl.BlockSpec(memory_space=pl.ANY)
VMEM = pl.BlockSpec(memory_space=pltpu.VMEM)


def local_kernel(name, kernel, out_shape, in_specs, scratch):
    return pl.pallas_call(
        kernel,
        out_shape=out_shape,
        in_specs=in_specs,
        out_specs=VMEM,
        scratch_shapes=scratch,
        name=name,
    )


def by_rows(array):
    return with_layout_constraint(array, Layout(tuple(range(array.ndim))))


def exchanged(pieces, axis):
    return lax.all_to_all(pieces, axis, split_axis=0, concat_axis=0, tiled=True)


def coded(values):
    root = jnp.sqrt(jnp.abs(values)) * ROOT_SCALE
    return jnp.where(values < 0, -root, root).astype(jnp.float16)


def decoded(codes):
    root = codes.astype(jnp.float32) * (1.0 / ROOT_SCALE)
    return root * jnp.abs(root)


def sketched(samples_hbm, sketch_hbm, out_ref, samples_ref, sketch_ref, held, arrivals):
    blocks = sketch_ref.shape[0]
    rows = samples_ref.shape[0]
    reach, width = out_ref.shape
    order = list(reversed(range(blocks)))
    loads = {j: pltpu.make_async_copy(sketch_hbm.at[j], sketch_ref.at[j], arrivals.at[j]) for j in order}
    first = pltpu.make_async_copy(samples_hbm, samples_ref, arrivals.at[blocks])
    first.start()
    for j in order:
        loads[j].start()
    for j in range(blocks):
        held[j, :EDGE] = jnp.zeros((EDGE, width), jnp.float32)
        held[j, EDGE + rows :] = jnp.zeros((held.shape[1] - EDGE - rows, width), jnp.float32)
    first.wait()
    for j in order:
        loads[j].wait()
        held[j, EDGE : EDGE + rows] = jnp.dot(
            samples_ref[...], sketch_ref[j], preferred_element_type=jnp.float32
        )
    total = held[blocks - 1, EDGE : EDGE + reach]
    for j in range(blocks - 1):
        start = EDGE - (blocks - 1 - j)
        total = total + held[j, start : start + reach]
    out_ref[...] = total


def correlated(
    block_rows, scale, own_hbm, other_hbm, tail_hbm, sums_ref, out_ref, turned, held, high, low, arrivals
):
    cores, reach, width = sums_ref.shape
    rows = own_hbm.shape[1]
    ends = tail_hbm.shape[1]
    core = lax.axis_index("core")
    mine = pl.ds(pl.multiple_of(core * rows, rows), rows)
    theirs = pl.ds(pl.multiple_of((cores - 1 - core) * rows, rows), rows)
    loads = [
        pltpu.make_async_copy(own_hbm, turned.at[:, mine], arrivals.at[0]),
        pltpu.make_async_copy(other_hbm, turned.at[:, theirs], arrivals.at[1]),
        pltpu.make_async_copy(tail_hbm, turned.at[:, cores * rows : cores * rows + ends], arrivals.at[2]),
    ]
    for load in loads:
        load.start()
    depth = cores * rows + 2 * EDGE
    held[:EDGE] = jnp.zeros((EDGE, width), jnp.float32)
    held[EDGE + reach :] = jnp.zeros((held.shape[0] - EDGE - reach, width), jnp.float32)
    held[EDGE : EDGE + reach] = sums_ref[0]
    for k in range(1, cores):
        start = EDGE + k * rows
        held[start : start + reach] = held[start : start + reach] + sums_ref[k]
    for sums in (high, low):
        sums[depth:] = jnp.zeros((sums.shape[0] - depth, sums.shape[1]), jnp.bfloat16)
    for i in range(block_rows):
        wide = held[EDGE - 1 - i : EDGE - 1 - i + depth]
        part = wide.astype(jnp.bfloat16)
        high[:depth, i * width : (i + 1) * width] = part
        low[:depth, i * width : (i + 1) * width] = (wide - part.astype(jnp.float32)).astype(jnp.bfloat16)
    for load in loads:
        load.wait()
    step = 2 * width
    for i in range(0, block_rows * width, step):
        found = jnp.dot(turned[...], high[:, i : i + step], preferred_element_type=jnp.float32)
        found = found + jnp.dot(turned[...], low[:, i : i + step], preferred_element_type=jnp.float32)
        out_ref[:, i : i + step] = (found * scale).astype(out_ref.dtype)


def shards(samples, sketch):
    rows, local = samples.shape
    blocks, _, width = sketch.shape
    cores = lax.axis_size("core")
    near = lax.axis_size(CHAN)
    groups = lax.axis_size(TM)
    half = width // cores
    part = -(-(rows + blocks - 1) // (near * EDGE)) * EDGE
    reach = near * part
    swap = [(i, cores - 1 - i) for i in range(cores)]
    ahead_route = [(i + cores, i) for i in range(groups - cores)]

    with jax.named_scope("swap"):
        other = by_rows(lax.ppermute(samples, "core", swap))
    partial = local_kernel(
        "sketched",
        sketched,
        jax.ShapeDtypeStruct((reach, width), jnp.float32),
        [ANY, ANY],
        [
            pltpu.VMEM(samples.shape, samples.dtype),
            pltpu.VMEM(sketch.shape, sketch.dtype),
            pltpu.VMEM((blocks, reach + 2 * EDGE, width), jnp.float32),
            pltpu.SemaphoreType.DMA((blocks + 1,)),
        ],
    )(samples, sketch)
    partial, other = lax.optimization_barrier((partial, other))
    with jax.named_scope("ahead"):
        first = lax.axis_index("core") == 0
        ahead = lax.ppermute(jnp.where(first, samples[:EDGE], other[:EDGE]), TM, ahead_route)
    with jax.named_scope("reduce"):
        arrived = exchanged(coded(partial).reshape(near, part, width), CHAN)
    arrived, ahead = lax.optimization_barrier((arrived, ahead))
    total = coded(decoded(arrived).sum(0))
    copies = [
        jnp.broadcast_to(total[None, :, k * half : (k + 1) * half], (near, part, half))
        for k in range(cores)
    ]
    with jax.named_scope("gather"):
        sums = exchanged(jnp.concatenate(copies, 0), ("core", *CHAN))
    tail = jnp.pad(ahead, ((0, LANES - EDGE), (0, 0)))
    scale = 1.0 / (rows * groups) ** 0.5
    found = local_kernel(
        "correlated",
        functools.partial(correlated, blocks, scale),
        jax.ShapeDtypeStruct((local, blocks * half), jnp.bfloat16),
        [ANY, ANY, ANY, VMEM],
        [
            pltpu.VMEM((local, cores * rows + LANES), samples.dtype),
            pltpu.VMEM((EDGE + (cores - 1) * rows + reach + 2 * EDGE, half), jnp.float32),
            pltpu.VMEM((cores * rows + LANES, blocks * half), jnp.bfloat16),
            pltpu.VMEM((cores * rows + LANES, blocks * half), jnp.bfloat16),
            pltpu.SemaphoreType.DMA((3,)),
        ],
    )(samples.T, other.T, tail.T, decoded(sums).reshape(cores, reach, half))
    with jax.named_scope("scatter"):
        landed = exchanged(found.reshape(groups, local // groups, blocks * half), TM)
    landed = landed.reshape(groups // cores, cores, local // groups, blocks, half)
    mine = landed.astype(jnp.float32).sum(0)
    return jnp.concatenate([mine[k] for k in range(cores)], -1)[None]


def solution(mesh):
    sizes = {"y_hi": 4, "z": 8, "core": 2, "y_lo": 2, "x": 4}
    fine = Mesh(mesh.devices.reshape(tuple(sizes.values())), tuple(sizes))
    placed = (P(TM, CHAN), P(None, CHAN, None))
    return jax.shard_map(
        shards, mesh=fine, in_specs=placed, out_specs=P(CHAN, TM, None, None), check_vma=False
    )
```

time: 83.6 us -> 82.7 us (0.989)
  starting transfers between devices: 14.6 us -> 19.7 us
  waiting for transfers between devices: 15.6 us -> 11 us
  blocking collectives: 37 us -> 35.5 us
  other arithmetic: 2.85 us -> 4.02 us
    all_to_all x2, waiting for transfers between devices: 12.4 us -> 5.37 us  [exchanged(): return lax.all_to_all(pieces, axis, split_axis=0, concat_axis=0, tiled=True)]
    ppermute x2, starting transfers between devices: 6.51 us -> 10 us  [the longest x1 8.74 us: shards(): other = by_rows(lax.ppermute(samples, 'core', swap))]
    ppermute x2, waiting for transfers between devices: 3.17 us -> 5.64 us  [the longest x1 5.63 us: shards(): lax.ppermute(jnp.where(first, samples[:EDGE], other[:EDGE]), TM, ahead_ro...]
    all_to_all x2, starting transfers between devices: 8.06 us -> 9.64 us  [exchanged(): return lax.all_to_all(pieces, axis, split_axis=0, concat_axis=0, tiled=True)]
    all_to_all x1, blocking collectives: 37 us -> 35.5 us  [exchanged(): return lax.all_to_all(pieces, axis, split_axis=0, concat_axis=0, tiled=True)]
    convert_element_type x2, other arithmetic: 1 us -> 2.13 us  [coded(): return jnp.where(values < 0, -root, root).astype(jnp.float16)]
    slice x4 -> x0, local copies, waits for them, and re-layouts: 1.02 us -> none  [the longest x2 0.86 us: shards(): head = lax.ppermute(samples[:EDGE], TM, route)]
    transpose x2 -> x1, local copies, waits for them, and re-layouts: 1.55 us -> 0.67 us  [shards(): found = local_kernel('correlated', functools.partial(correlated, blocks,...]
  transfers between devices with their start and end apart: 4 -> 4, of which waited for: 3 -> 2; matrix products, arithmetic and copies ran while one was open for 4% -> 3% of each run, Pallas kernels for 4% -> 4%
where the time goes in v3:
time: 82.7 us; the launch traced here: 82.2 us
  blocking collectives  35.5 us (43%)
  starting transfers between devices  19.7 us (24%)
  waiting for transfers between devices  11 us (13%)
  Pallas kernels  8.29 us (10%)
  other arithmetic  4.02 us (5%)
  local copies, waits for them, and re-layouts  3.56 us (4%)
    all_to_all x1, blocking collectives, exchanged(): return lax.all_to_all(pieces, axis, split_axis=0, concat_axis=0, tiled=True)  35.5 us
    all_to_all x2, starting transfers between devices, exchanged(): return lax.all_to_all(pieces, axis, split_axis=0, concat_axis=0, tiled=True)  9.64 us
    ppermute x1, starting transfers between devices, shards(): other = by_rows(lax.ppermute(samples, 'core', swap))  8.74 us
    ppermute x1, waiting for transfers between devices, shards(): lax.ppermute(jnp.where(first, samples[:EDGE], other[:EDGE]), TM, ahead_ro...  5.63 us
    all_to_all x2, waiting for transfers between devices, exchanged(): return lax.all_to_all(pieces, axis, split_axis=0, concat_axis=0, tiled=True)  5.37 us
    pallas_call x1, Pallas kernels, shards(): local_kernel('correlated', functools.partial(correlated, blocks, scale),...  4.63 us
    pallas_call x1, Pallas kernels, shards(): local_kernel('sketched', sketched, jax.ShapeDtypeStruct((reach, width), j...  3.66 us
    convert_element_type x2, other arithmetic, coded(): return jnp.where(values < 0, -root, root).astype(jnp.float16)  2.13 us
  transfers between devices with their start and end apart: 4, of which 2 were waited for; matrix products, arithmetic and copies ran while one was open for 3% of the time, Pallas kernels for 4%

profile of v3, /device:TPU:1, one launch (start us, length us, event | category | flops | bytes accessed | tf_op | source)
XLA Modules:
  0.0 82.2 jit_solution(6835780732159674607)
XLA Ops:
  0.0 8.7 %collective-permute-start = (bf16[512,512]{1,0:T(8,128)(2,1)}, bf16[512,512]{1,0:T(8,128)(2,1)S(1)}, u32[]{:S(2)}, u32[]{:S(2)}) collective-permute-start(bf16[512,512]{1,0:T(8,128)(2,1)} %samples_hbm.1), channel_id=1, source_target_pairs={{0,8},{8,0},{1,9},{9,1},{2,10},{10,2},{3,11},{11,3},{4,12},{12,4},... | collective-permute-start | bytes 1572872 | tf_op jit(solution)/shard_map/swap/ppermute | solution.py:128
  8.7 3.7 %sketched.1 = f32[576,256]{1,0:T(8,128)} custom-call(bf16[512,512]{1,0:T(8,128)(2,1)} %samples_hbm.1, bf16[4,512,256]{2,1,0:T(8,128)(2,1)} %sketch_hbm.1), custom_call_target="tpu_custom_call" | custom-call | tf_op jit(solution)/shard_map/sketched/pallas_call | solution.py:129
  12.4 0.0 copy-start
  12.4 0.0 collective-permute-done
  12.4 2.1 %fusion = f16[576,256]{1,0:T(8,128)(2,1)} fusion(f32[576,256]{1,0:T(8,128)} %sketched.1), kind=kLoop, calls=%fused_computation.4 | loop fusion | flops 884736 | bytes 884736 | tf_op jit(solution)/shard_map/reduce/convert_element_type | solution.py:42
  14.5 3.4 %all-to-all-start = ((f16[8,72,256]{2,1,0:T(8,128)(2,1)}), f16[8,72,256]{2,1,0:T(8,128)(2,1)S(1)}, u32[]{:S(2)}, u32[]{:S(2)}) async-start(f16[8,72,256]{2,1,0:T(8,128)(2,1)} %bitcast.2), calls=%async_computation | async-start | bytes 589824 | tf_op jit(solution)/shard_map/reduce/all_to_all | solution.py:37
  18.0 0.0 copy-done
  18.0 0.2 copy.14
  18.1 1.3 %collective-permute-start.1 = (bf16[8,512]{0,1:T(8,128)(2,1)S(1)}, bf16[8,512]{0,1:T(8,128)(2,1)S(1)}, u32[]{:S(2)}, u32[]{:S(2)}) collective-permute-start(bf16[8,512]{0,1:T(8,128)(2,1)S(1)} %copy.14), channel_id=1, source_target_pairs={{16,0},{24,8},{32,16},{40,24},{48,32},{56,40},{64,48},{72,56},{80,... | collective-permute-start | bytes 24584 | tf_op jit(solution)/shard_map/ahead/ppermute | solution.py:144
  19.4 5.6 %collective-permute-done.1 = bf16[8,512]{0,1:T(8,128)(2,1)S(1)} collective-permute-done((bf16[8,512]{0,1:T(8,128)(2,1)S(1)}, bf16[8,512]{0,1:T(8,128)(2,1)S(1)}, u32[]{:S(2)}, u32[]{:S(2)}) %collective-permute-start.1) | collective-permute-done | bytes 8224 | tf_op jit(solution)/shard_map/ahead/ppermute | solution.py:144
  25.1 0.0 all-to-all-done
  25.1 0.1 fusion.1
  25.3 0.8 pad_maximum_fusion
  26.1 6.2 %all-to-all-start.1 = ((f16[16,72,128]{2,1,0:T(8,128)(2,1)}), f16[16,72,128]{2,1,0:T(8,128)(2,1)S(1)}, u32[]{:S(2)}, u32[]{:S(2)}) async-start(f16[16,72,128]{2,1,0:T(8,128)(2,1)} %pad_maximum_fusion), calls=%async_computation.1 | async-start | bytes 589824 | tf_op jit(solution)/shard_map/gather/all_to_all | solution.py:37
  32.3 1.0 %copy.12 = bf16[512,512]{0,1:T(8,128)(2,1)} copy(bf16[512,512]{1,0:T(8,128)(2,1)S(1)} %copy-done) | data formatting | bytes 1048576 | tf_op args[0]
  33.3 1.0 %copy.13 = bf16[512,512]{0,1:T(8,128)(2,1)} copy(bf16[512,512]{1,0:T(8,128)(2,1)S(1)} %collective-permute-done) | data formatting | bytes 1048576 | tf_op jit(solution)/shard_map/optimization_barrier | solution.py:141
  34.4 0.7 pad_bitcast_fusion.tail_hbm
  35.0 5.4 %all-to-all-done.1 = f16[16,72,128]{2,1,0:T(8,128)(2,1)S(1)} async-done(((f16[16,72,128]{2,1,0:T(8,128)(2,1)}), f16[16,72,128]{2,1,0:T(8,128)(2,1)S(1)}, u32[]{:S(2)}, u32[]{:S(2)}) %all-to-all-start.1) | async-done | bytes 294944 | tf_op jit(solution)/shard_map/gather/all_to_all | solution.py:37
  40.4 0.9 %abs_multiply_fusion = f32[16,72,128]{2,1,0:T(8,128)} fusion(f16[16,72,128]{2,1,0:T(8,128)(2,1)S(1)} %all-to-all-done.1), kind=kLoop, calls=%fused_computation.1 | loop fusion | flops 589824 | bytes 884736 | tf_op jit(solution)/shard_map/mul | solution.py:47
  41.3 4.6 %correlated.1 = bf16[512,512]{1,0:T(8,128)(2,1)} custom-call(bf16[512,512]{1,0:T(8,128)(2,1)} %bitcast.17, bf16[512,512]{1,0:T(8,128)(2,1)} %bitcast.18, bf16[512,128]{1,0:T(8,128)(2,1)} %pad_bitcast_fusion.tail_hbm, f32[2,576,128]{2,1,0:T(8,128)} %bitcast.15), custom_call_target="tpu_custom_call" | custom-call | tf_op jit(solution)/shard_map/correlated/pallas_call | solution.py:157
  45.9 35.5 %all_to_all.15 = bf16[64,8,512]{2,1,0:T(8,128)(2,1)S(1)} all-to-all(bf16[64,8,512]{2,1,0:T(8,128)(2,1)} %bitcast.19), channel_id=1, replica_groups=mesh['y_hi'=4,'z'=8,'core'=2,'y_lo'=2,'x'=4] {'y_hi','z','core'}, dimensions={0} | all-to-all | bytes 1048576 | tf_op jit(solution)/shard_map/scatter/all_to_all | solution.py:37
  81.4 0.1 convert_reduce_fusion
  81.5 0.6 copy.15
  (7 shorter events, 0.1 us)
Async XLA Ops:
  0.0 12.4 %collective-permute-start = (bf16[512,512]{1,0:T(8,128)(2,1)}, bf16[512,512]{1,0:T(8,128)(2,1)S(1)}, u32[]{:S(2)}, u32[]{:S(2)}) collective-permute-start(bf16[512,512]{1,0:T(8,128)(2,1)} %samples_hbm.1), channel_id=1, source_target_pairs={{0,8},{8,0},{1,9},{9,1},{2,10},{10,2},{3,11},{11,3},{4,12},{12,4},... | collective-permute-start | bytes 1572872 | tf_op jit(solution)/shard_map/swap/ppermute | solution.py:128
  12.4 5.6 %copy-start = (bf16[512,512]{1,0:T(8,128)(2,1)S(1)}, bf16[512,512]{1,0:T(8,128)(2,1)}, u32[]{:S(2)}) copy-start(bf16[512,512]{1,0:T(8,128)(2,1)} %samples_hbm.1) | copy-start | bytes 1572868
  14.5 10.6 %all-to-all-start = ((f16[8,72,256]{2,1,0:T(8,128)(2,1)}), f16[8,72,256]{2,1,0:T(8,128)(2,1)S(1)}, u32[]{:S(2)}, u32[]{:S(2)}) async-start(f16[8,72,256]{2,1,0:T(8,128)(2,1)} %bitcast.2), calls=%async_computation | async-start | bytes 589824 | tf_op jit(solution)/shard_map/reduce/all_to_all | solution.py:37
  18.1 6.9 %collective-permute-start.1 = (bf16[8,512]{0,1:T(8,128)(2,1)S(1)}, bf16[8,512]{0,1:T(8,128)(2,1)S(1)}, u32[]{:S(2)}, u32[]{:S(2)}) collective-permute-start(bf16[8,512]{0,1:T(8,128)(2,1)S(1)} %copy.14), channel_id=1, source_target_pairs={{16,0},{24,8},{32,16},{40,24},{48,32},{56,40},{64,48},{72,56},{80,... | collective-permute-start | bytes 24584 | tf_op jit(solution)/shard_map/ahead/ppermute | solution.py:144
  26.1 14.3 %all-to-all-start.1 = ((f16[16,72,128]{2,1,0:T(8,128)(2,1)}), f16[16,72,128]{2,1,0:T(8,128)(2,1)S(1)}, u32[]{:S(2)}, u32[]{:S(2)}) async-start(f16[16,72,128]{2,1,0:T(8,128)(2,1)} %pad_maximum_fusion), calls=%async_computation.1 | async-start | bytes 589824 | tf_op jit(solution)/shard_map/gather/all_to_all | solution.py:37

commit v4 on v3

--- a/solution.py
+++ b/solution.py
@@ -14,19 +14,22 @@
 EDGE = 8
 LANES = 128
 ROOT_SCALE = 512.0
-ANY = pl.BlockSpec(memory_space=pl.ANY)
 VMEM = pl.BlockSpec(memory_space=pltpu.VMEM)
 
 
-def local_kernel(name, kernel, out_shape, in_specs, scratch):
-    return pl.pallas_call(
-        kernel,
-        out_shape=out_shape,
-        in_specs=in_specs,
-        out_specs=VMEM,
-        scratch_shapes=scratch,
-        name=name,
-    )
+def local_kernel(name, kernel, shape, dtype, scratch):
+    def call(*args):
+        args = [pltpu.with_memory_space_constraint(a, pltpu.VMEM) for a in args]
+        return pl.pallas_call(
+            kernel,
+            out_shape=pltpu.VMEM(shape, dtype),
+            in_specs=[VMEM] * len(args),
+            out_specs=VMEM,
+            scratch_shapes=scratch,
+            name=name,
+        )(*args)
+
+    return call
 
 
 def by_rows(array):
@@ -47,22 +50,13 @@
     return root * jnp.abs(root)
 
 
-def sketched(samples_hbm, sketch_hbm, out_ref, samples_ref, sketch_ref, held, arrivals):
+def sketched(samples_ref, sketch_ref, out_ref, held):
     blocks = sketch_ref.shape[0]
     rows = samples_ref.shape[0]
     reach, width = out_ref.shape
-    order = list(reversed(range(blocks)))
-    loads = {j: pltpu.make_async_copy(sketch_hbm.at[j], sketch_ref.at[j], arrivals.at[j]) for j in order}
-    first = pltpu.make_async_copy(samples_hbm, samples_ref, arrivals.at[blocks])
-    first.start()
-    for j in order:
-        loads[j].start()
     for j in range(blocks):
         held[j, :EDGE] = jnp.zeros((EDGE, width), jnp.float32)
         held[j, EDGE + rows :] = jnp.zeros((held.shape[1] - EDGE - rows, width), jnp.float32)
-    first.wait()
-    for j in order:
-        loads[j].wait()
         held[j, EDGE : EDGE + rows] = jnp.dot(
             samples_ref[...], sketch_ref[j], preferred_element_type=jnp.float32
         )
@@ -73,22 +67,13 @@
     out_ref[...] = total
 
 
-def correlated(
-    block_rows, scale, own_hbm, other_hbm, tail_hbm, sums_ref, out_ref, turned, held, high, low, arrivals
-):
+def correlated(block_rows, scale, own_ref, other_ref, tail_ref, sums_ref, out_ref, held, high, low):
     cores, reach, width = sums_ref.shape
-    rows = own_hbm.shape[1]
-    ends = tail_hbm.shape[1]
+    rows = own_ref.shape[1]
     core = lax.axis_index("core")
     mine = pl.ds(pl.multiple_of(core * rows, rows), rows)
     theirs = pl.ds(pl.multiple_of((cores - 1 - core) * rows, rows), rows)
-    loads = [
-        pltpu.make_async_copy(own_hbm, turned.at[:, mine], arrivals.at[0]),
-        pltpu.make_async_copy(other_hbm, turned.at[:, theirs], arrivals.at[1]),
-        pltpu.make_async_copy(tail_hbm, turned.at[:, cores * rows : cores * rows + ends], arrivals.at[2]),
-    ]
-    for load in loads:
-        load.start()
+    ends = pl.ds(cores * rows, tail_ref.shape[1])
     depth = cores * rows + 2 * EDGE
     held[:EDGE] = jnp.zeros((EDGE, width), jnp.float32)
     held[EDGE + reach :] = jnp.zeros((held.shape[0] - EDGE - reach, width), jnp.float32)
@@ -103,12 +88,14 @@
         part = wide.astype(jnp.bfloat16)
         high[:depth, i * width : (i + 1) * width] = part
         low[:depth, i * width : (i + 1) * width] = (wide - part.astype(jnp.float32)).astype(jnp.bfloat16)
-    for load in loads:
-        load.wait()
     step = 2 * width
     for i in range(0, block_rows * width, step):
-        found = jnp.dot(turned[...], high[:, i : i + step], preferred_element_type=jnp.float32)
-        found = found + jnp.dot(turned[...], low[:, i : i + step], preferred_element_type=jnp.float32)
+        found = jnp.zeros((out_ref.shape[0], step), jnp.float32)
+        for turned, where in ((own_ref, mine), (other_ref, theirs), (tail_ref, ends)):
+            for sums in (high, low):
+                found = found + jnp.dot(
+                    turned[...], sums[where, i : i + step], preferred_element_type=jnp.float32
+                )
         out_ref[:, i : i + step] = (found * scale).astype(out_ref.dtype)
 
 
@@ -129,14 +116,9 @@
     partial = local_kernel(
         "sketched",
         sketched,
-        jax.ShapeDtypeStruct((reach, width), jnp.float32),
-        [ANY, ANY],
-        [
-            pltpu.VMEM(samples.shape, samples.dtype),
-            pltpu.VMEM(sketch.shape, sketch.dtype),
-            pltpu.VMEM((blocks, reach + 2 * EDGE, width), jnp.float32),
-            pltpu.SemaphoreType.DMA((blocks + 1,)),
-        ],
+        (reach, width),
+        jnp.float32,
+        [pltpu.VMEM((blocks, reach + 2 * EDGE, width), jnp.float32)],
     )(samples, sketch)
     partial, other = lax.optimization_barrier((partial, other))
     with jax.named_scope("ahead"):
@@ -157,14 +139,12 @@
     found = local_kernel(
         "correlated",
         functools.partial(correlated, blocks, scale),
-        jax.ShapeDtypeStruct((local, blocks * half), jnp.bfloat16),
-        [ANY, ANY, ANY, VMEM],
+        (local, blocks * half),
+        jnp.bfloat16,
         [
-            pltpu.VMEM((local, cores * rows + LANES), samples.dtype),
             pltpu.VMEM((EDGE + (cores - 1) * rows + reach + 2 * EDGE, half), jnp.float32),
             pltpu.VMEM((cores * rows + LANES, blocks * half), jnp.bfloat16),
             pltpu.VMEM((cores * rows + LANES, blocks * half), jnp.bfloat16),
-            pltpu.SemaphoreType.DMA((3,)),
         ],
     )(samples.T, other.T, tail.T, decoded(sums).reshape(cores, reach, half))
     with jax.named_scope("scatter"):

time: 82.7 us -> 77.1 us (0.932)
  Pallas kernels: 8.29 us -> 2.67 us
  waiting for transfers between devices: 11 us -> 13.2 us
  other arithmetic: 4.02 us -> 2.08 us
    pallas_call x2, Pallas kernels: 8.29 us -> 2.67 us  [call(): pl.pallas_call(kernel, out_shape=pltpu.VMEM(shape, dtype), in_specs=[VMEM...]
    all_to_all x2, waiting for transfers between devices: 5.37 us -> 7.6 us  [exchanged(): return lax.all_to_all(pieces, axis, split_axis=0, concat_axis=0, tiled=True)]
    unnamed x3 -> x5, local copies, waits for them, and re-layouts: 1.01 us -> 2.47 us
    convert_element_type x2, other arithmetic: 2.13 us -> 1.01 us  [coded(): return jnp.where(values < 0, -root, root).astype(jnp.float16)]
  transfers between devices with their start and end apart: 4 -> 4, of which waited for: 2 -> 2; matrix products, arithmetic and copies ran while one was open for 3% -> 1% of each run, Pallas kernels for 4% -> 1%
where the time goes in v4:
time: 77.1 us; the launch traced here: 76.6 us
  blocking collectives  35.3 us (46%)
  starting transfers between devices  19.7 us (26%)
  waiting for transfers between devices  13.2 us (17%)
  local copies, waits for them, and re-layouts  3.56 us (5%)
  Pallas kernels  2.67 us (3%)
  other arithmetic  2.08 us (3%)
    all_to_all x1, blocking collectives, exchanged(): return lax.all_to_all(pieces, axis, split_axis=0, concat_axis=0, tiled=True)  35.3 us
    all_to_all x2, starting transfers between devices, exchanged(): return lax.all_to_all(pieces, axis, split_axis=0, concat_axis=0, tiled=True)  9.65 us
    ppermute x1, starting transfers between devices, shards(): other = by_rows(lax.ppermute(samples, 'core', swap))  8.73 us
    all_to_all x2, waiting for transfers between devices, exchanged(): return lax.all_to_all(pieces, axis, split_axis=0, concat_axis=0, tiled=True)  7.6 us
    ppermute x1, waiting for transfers between devices, shards(): lax.ppermute(jnp.where(first, samples[:EDGE], other[:EDGE]), TM, ahead_ro...  5.64 us
    pallas_call x2, Pallas kernels, call(): pl.pallas_call(kernel, out_shape=pltpu.VMEM(shape, dtype), in_specs=[VMEM...  2.67 us
    unnamed x5, local copies, waits for them, and re-layouts  2.47 us
  transfers between devices with their start and end apart: 4, of which 2 were waited for; matrix products, arithmetic and copies ran while one was open for 1% of the time, Pallas kernels for 1%

profile of v4, /device:TPU:1, one launch (start us, length us, event | category | flops | bytes accessed | tf_op | source)
XLA Modules:
  0.0 76.6 jit_solution(349666899375573744)
XLA Ops:
  0.0 8.7 %collective-permute-start = (bf16[512,512]{1,0:T(8,128)(2,1)}, bf16[512,512]{1,0:T(8,128)(2,1)S(1)}, u32[]{:S(2)}, u32[]{:S(2)}) collective-permute-start(bf16[512,512]{1,0:T(8,128)(2,1)} %samples_ref.1), channel_id=1, source_target_pairs={{0,8},{8,0},{1,9},{9,1},{2,10},{10,2},{3,11},{11,3},{4,12},{12,4},... | collective-permute-start | bytes 1572872 | tf_op jit(solution)/shard_map/swap/ppermute | solution.py:115
  8.7 0.0 copy-start
  8.8 1.0 %copy-done = bf16[512,512]{1,0:T(8,128)(2,1)S(1)} copy-done((bf16[512,512]{1,0:T(8,128)(2,1)S(1)}, bf16[512,512]{1,0:T(8,128)(2,1)}, u32[]{:S(2)}) %copy-start) | copy-done | bytes 524312
  9.8 0.0 copy-start.1
  9.8 1.2 %copy-done.1 = bf16[4,512,256]{2,1,0:T(8,128)(2,1)S(1)} copy-done((bf16[4,512,256]{2,1,0:T(8,128)(2,1)S(1)}, bf16[4,512,256]{2,1,0:T(8,128)(2,1)}, u32[]{:S(2)}) %copy-start.1) | copy-done | bytes 1048600
  11.0 0.7 sketched.1
  11.7 0.0 collective-permute-done
  11.7 1.0 %fusion = f16[576,256]{1,0:T(8,128)(2,1)} fusion(f32[576,256]{1,0:T(8,128)S(1)} %sketched.1), kind=kLoop, calls=%fused_computation.4 | loop fusion | flops 884736 | bytes 884736 | tf_op jit(solution)/shard_map/reduce/convert_element_type | solution.py:45
  12.7 3.4 %all-to-all-start = ((f16[8,72,256]{2,1,0:T(8,128)(2,1)}), f16[8,72,256]{2,1,0:T(8,128)(2,1)S(1)}, u32[]{:S(2)}, u32[]{:S(2)}) async-start(f16[8,72,256]{2,1,0:T(8,128)(2,1)} %bitcast.2), calls=%async_computation | async-start | bytes 589824 | tf_op jit(solution)/shard_map/reduce/all_to_all | solution.py:40
  16.2 0.2 copy.14
  16.3 1.3 %collective-permute-start.1 = (bf16[8,512]{0,1:T(8,128)(2,1)S(1)}, bf16[8,512]{0,1:T(8,128)(2,1)S(1)}, u32[]{:S(2)}, u32[]{:S(2)}) collective-permute-start(bf16[8,512]{0,1:T(8,128)(2,1)S(1)} %copy.14), channel_id=1, source_target_pairs={{16,0},{24,8},{32,16},{40,24},{48,32},{56,40},{64,48},{72,56},{80,... | collective-permute-start | bytes 24584 | tf_op jit(solution)/shard_map/ahead/ppermute | solution.py:126
  17.6 5.6 %collective-permute-done.1 = bf16[8,512]{0,1:T(8,128)(2,1)S(1)} collective-permute-done((bf16[8,512]{0,1:T(8,128)(2,1)S(1)}, bf16[8,512]{0,1:T(8,128)(2,1)S(1)}, u32[]{:S(2)}, u32[]{:S(2)}) %collective-permute-start.1) | collective-permute-done | bytes 8224 | tf_op jit(solution)/shard_map/ahead/ppermute | solution.py:126
  23.3 0.0 all-to-all-done
  23.3 0.1 fusion.1
  23.5 0.8 %pad_maximum_fusion = f16[16,72,128]{2,1,0:T(8,128)(2,1)} fusion(f16[8,72,128]{2,1,0:T(8,128)(2,1)S(1)} %broadcast_in_dim.7, f16[8,72,128]{2,1,0:T(8,128)(2,1)S(1)} %broadcast_in_dim.6), kind=kLoop, calls=%fused_computation.6 | loop fusion | flops 147456 | bytes 589824 | tf_op jit(solution)/shard_map/gather/concatenate | solution.py:136
  24.3 6.2 %all-to-all-start.1 = ((f16[16,72,128]{2,1,0:T(8,128)(2,1)}), f16[16,72,128]{2,1,0:T(8,128)(2,1)S(1)}, u32[]{:S(2)}, u32[]{:S(2)}) async-start(f16[16,72,128]{2,1,0:T(8,128)(2,1)} %pad_maximum_fusion), calls=%async_computation.1 | async-start | bytes 589824 | tf_op jit(solution)/shard_map/gather/all_to_all | solution.py:40
  30.5 0.2 copy.12
  30.7 0.2 copy.13
  31.0 7.6 %all-to-all-done.1 = f16[16,72,128]{2,1,0:T(8,128)(2,1)S(1)} async-done(((f16[16,72,128]{2,1,0:T(8,128)(2,1)}), f16[16,72,128]{2,1,0:T(8,128)(2,1)S(1)}, u32[]{:S(2)}, u32[]{:S(2)}) %all-to-all-start.1) | async-done | bytes 294944 | tf_op jit(solution)/shard_map/gather/all_to_all | solution.py:40
  38.6 0.1 abs_multiply_fusion
  38.7 2.0 %correlated.1 = bf16[512,512]{1,0:T(8,128)(2,1)S(1)} custom-call(bf16[512,512]{1,0:T(8,128)(2,1)S(1)} %bitcast.16, bf16[512,512]{1,0:T(8,128)(2,1)S(1)} %bitcast.17, bf16[512,128]{1,0:T(8,128)(2,1)S(1)} %pad_bitcast_fusion.tail_ref, f32[2,576,128]{2,1,0:T(8,128)S(1)} %bitcast.15), custom_call_target="tpu_custom_call" | custom-call | tf_op jit(solution)/shard_map/correlated/pallas_call | solution.py:23
  40.6 35.3 %all_to_all.15 = bf16[64,8,512]{2,1,0:T(8,128)(2,1)S(1)} all-to-all(bf16[64,8,512]{2,1,0:T(8,128)(2,1)S(1)} %bitcast.18), channel_id=1, replica_groups=mesh['y_hi'=4,'z'=8,'core'=2,'y_lo'=2,'x'=4] {'y_hi','z','core'}, dimensions={0} | all-to-all | bytes 1048576 | tf_op jit(solution)/shard_map/scatter/all_to_all | solution.py:40
  75.9 0.1 convert_reduce_fusion
  76.0 0.6 copy.15
  (8 shorter events, 0.1 us)
Async XLA Ops:
  0.0 11.7 %collective-permute-start = (bf16[512,512]{1,0:T(8,128)(2,1)}, bf16[512,512]{1,0:T(8,128)(2,1)S(1)}, u32[]{:S(2)}, u32[]{:S(2)}) collective-permute-start(bf16[512,512]{1,0:T(8,128)(2,1)} %samples_ref.1), channel_id=1, source_target_pairs={{0,8},{8,0},{1,9},{9,1},{2,10},{10,2},{3,11},{11,3},{4,12},{12,4},... | collective-permute-start | bytes 1572872 | tf_op jit(solution)/shard_map/swap/ppermute | solution.py:115
  8.7 1.0 %copy-start = (bf16[512,512]{1,0:T(8,128)(2,1)S(1)}, bf16[512,512]{1,0:T(8,128)(2,1)}, u32[]{:S(2)}) copy-start(bf16[512,512]{1,0:T(8,128)(2,1)} %samples_ref.1) | copy-start | bytes 1572868
  9.8 1.2 %copy-start.1 = (bf16[4,512,256]{2,1,0:T(8,128)(2,1)S(1)}, bf16[4,512,256]{2,1,0:T(8,128)(2,1)}, u32[]{:S(2)}) copy-start(bf16[4,512,256]{2,1,0:T(8,128)(2,1)} %sketch_ref.1) | copy-start | bytes 3145732
  12.7 10.6 %all-to-all-start = ((f16[8,72,256]{2,1,0:T(8,128)(2,1)}), f16[8,72,256]{2,1,0:T(8,128)(2,1)S(1)}, u32[]{:S(2)}, u32[]{:S(2)}) async-start(f16[8,72,256]{2,1,0:T(8,128)(2,1)} %bitcast.2), calls=%async_computation | async-start | bytes 589824 | tf_op jit(solution)/shard_map/reduce/all_to_all | solution.py:40
  16.3 6.9 %collective-permute-start.1 = (bf16[8,512]{0,1:T(8,128)(2,1)S(1)}, bf16[8,512]{0,1:T(8,128)(2,1)S(1)}, u32[]{:S(2)}, u32[]{:S(2)}) collective-permute-start(bf16[8,512]{0,1:T(8,128)(2,1)S(1)} %copy.14), channel_id=1, source_target_pairs={{16,0},{24,8},{32,16},{40,24},{48,32},{56,40},{64,48},{72,56},{80,... | collective-permute-start | bytes 24584 | tf_op jit(solution)/shard_map/ahead/ppermute | solution.py:126
  24.3 14.3 %all-to-all-start.1 = ((f16[16,72,128]{2,1,0:T(8,128)(2,1)}), f16[16,72,128]{2,1,0:T(8,128)(2,1)S(1)}, u32[]{:S(2)}, u32[]{:S(2)}) async-start(f16[16,72,128]{2,1,0:T(8,128)(2,1)} %pad_maximum_fusion), calls=%async_computation.1 | async-start | bytes 589824 | tf_op jit(solution)/shard_map/gather/all_to_all | solution.py:40
